TPU v7x, 32 devices: a whole 2x2x4 slice. The times are simulated.
32 devices in a mesh: seq: 8 (over y, x, core), red: 4 (over z).
Axes of the slice: x: 2, y: 2, z: 4, core: 2. Of those that a mesh axis runs over, the one named last changes fastest.
Arguments:
- token_ids: int32 [1024], P('seq'), may hold values from 0 to 511
- embedding: bfloat16 [512, 4096], P(None, 'red'), may hold values from -6 to 6
- proj_weight: bfloat16 [4096, 3, 4, 256], P('red', None, None, 'seq'), may hold values from -0.09375 to 0.09375
- filters: float32 [1024, 1024], P('seq', 'red'), may hold values from -1 to 1
- cotangent: float32 [1024, 1024], P('seq', 'red'), may hold values from -6 to 6
Outputs:
- output: float32 [1024, 1024], P('seq', 'red')
- filter_grad: float32 [1024, 1024], P('seq', 'red')
- branch_grads: bfloat16 [1024, 3, 1024], P('seq', None, 'red')
- weight_grad: float32 [4096, 3, 4, 256], P('red', None, None, 'seq')
All inputs are finite; a program needn't handle non-finite values.
Results may differ from a plain program's by a relative error of at most 0.0029.
Values sent between devices are 32-bit elements; how exact they have to be, the bound alone decides.
A program may use at most 64 MiB of HBM per device.

v0:
```python
import math
import jax
import jax.numpy as jnp
from jax import lax
from jax.sharding import PartitionSpec as P

precise_mode = lax.Precision.HIGHEST


def angles(numbers, modulus, direction):
    phase = (numbers % modulus).astype(jnp.float32) * (direction * 2.0 * math.pi / modulus)
    return (jnp.cos(phase), jnp.sin(phase))


def rotate(real_part, imag_part, cosine, sine_part):
    return (real_part * cosine - imag_part * sine_part, real_part * sine_part + imag_part * cosine)


def complex_einsum(formula, matrix, values):
    mat_real, mat_imag = matrix
    val_real, val_imag = values
    real_out = jnp.einsum(formula, mat_real, val_real, precision=precise_mode) - jnp.einsum(
        formula, mat_imag, val_imag, precision=precise_mode
    )
    imag_out = jnp.einsum(formula, mat_real, val_imag, precision=precise_mode) + jnp.einsum(
        formula, mat_imag, val_real, precision=precise_mode
    )
    return (real_out, imag_out)


def factors(length_total):
    first_factor = 1
    for candidate in range(1, math.isqrt(length_total) + 1):
        if length_total % candidate == 0:
            first_factor = candidate
    return (first_factor, length_total // first_factor)


def combine_spectra(spec_real, spec_imag, width):
    filt_re = spec_real[..., :width]
    inner_re = spec_real[..., width : 2 * width]
    up_re = spec_real[..., 2 * width :]
    filt_im = spec_imag[..., :width]
    inner_im = spec_imag[..., width : 2 * width]
    up_im = spec_imag[..., 2 * width :]
    joined_real = jnp.concatenate(
        [
            filt_re * inner_re - filt_im * inner_im,
            filt_re * up_re + filt_im * up_im,
            up_re * inner_re + up_im * inner_im,
        ],
        axis=-1,
    )
    joined_imag = jnp.concatenate(
        [
            filt_re * inner_im + filt_im * inner_re,
            filt_re * up_im - filt_im * up_re,
            up_im * inner_re - up_re * inner_im,
        ],
        axis=-1,
    )
    return (joined_real, joined_imag)


def local_convolve(signals):
    length, branch_count, narrow = signals.shape
    total = 2 * length
    first_factor, second_factor = factors(total)
    flat = signals.reshape(length, branch_count * narrow)
    padded = jnp.concatenate([flat, jnp.zeros_like(flat)], axis=0).reshape(
        first_factor, second_factor, branch_count * narrow
    )
    first_index = jnp.arange(first_factor, dtype=jnp.int32)
    second_index = jnp.arange(second_factor, dtype=jnp.int32)
    cosine, sine_part = angles(first_index[:, None] * first_index[None, :], first_factor, -1.0)
    real_part = jnp.einsum("kn,nbm->kbm", cosine, padded, precision=precise_mode)
    imag_part = jnp.einsum("kn,nbm->kbm", sine_part, padded, precision=precise_mode)
    cosine, sine_part = angles(first_index[:, None] * second_index[None, :], total, -1.0)
    real_part, imag_part = rotate(real_part, imag_part, cosine[:, :, None], sine_part[:, :, None])
    real_part, imag_part = complex_einsum(
        "lb,kbm->klm",
        angles(second_index[:, None] * second_index[None, :], second_factor, -1.0),
        (real_part, imag_part),
    )
    real_part, imag_part = combine_spectra(real_part, imag_part, narrow)
    real_part, imag_part = complex_einsum(
        "bl,klm->kbm",
        angles(second_index[:, None] * second_index[None, :], second_factor, 1.0),
        (real_part, imag_part),
    )
    cosine, sine_part = angles(first_index[:, None] * second_index[None, :], total, 1.0)
    real_part, imag_part = rotate(real_part, imag_part, cosine[:, :, None], sine_part[:, :, None])
    cosine, sine_part = angles(first_index[:, None] * first_index[None, :], first_factor, 1.0)
    result = jnp.einsum("nk,kbm->nbm", cosine, real_part, precision=precise_mode) - jnp.einsum(
        "nk,kbm->nbm", sine_part, imag_part, precision=precise_mode
    )
    result = result.reshape(total, branch_count * narrow)[:length] / total
    return result.reshape(length, branch_count, narrow)


def shards(token_ids, embedding, proj_weight, filters, cotangent):
    tok_count = token_ids.shape[0]
    devices = lax.axis_size("seq")
    width = filters.shape[1]
    vocabulary = embedding.shape[0]
    width_rows, branches, red_count, piece = proj_weight.shape
    scale_factor = float(tok_count * devices) ** (-0.5)
    table = jnp.dot(
        embedding,
        proj_weight.reshape(width_rows, branches * red_count * piece),
        preferred_element_type=jnp.float32,
    )
    table = table.reshape(vocabulary, branches, red_count, piece)
    own_table = lax.psum_scatter(table, "red", scatter_dimension=2, tiled=True)
    full_table = lax.all_gather(own_table, "seq", axis=3, tiled=True)
    projected = jnp.take(full_table, token_ids, axis=0)
    projected = projected.reshape(tok_count, branches, width)
    queries = projected[:, 0]
    key_rows = projected[:, 1]
    value_rows = projected[:, 2]
    inner = key_rows * value_rows
    upstream = cotangent * queries
    stacked = jnp.stack([filters, inner, upstream], axis=1)
    whole_length = lax.all_to_all(stacked, "seq", split_axis=2, concat_axis=0, tiled=True)
    results = local_convolve(whole_length)
    returned = lax.all_to_all(results, "seq", split_axis=0, concat_axis=2, tiled=True)
    conv = returned[:, 0]
    grad_inner = returned[:, 1]
    filter_raw = returned[:, 2]
    output = queries * conv
    filter_grad = filter_raw * scale_factor
    branch_grads = jnp.stack(
        [cotangent * conv, grad_inner * value_rows, grad_inner * key_rows], axis=1
    ).astype(jnp.bfloat16)
    one_hot = (token_ids[:, None] == lax.iota(jnp.int32, vocabulary)[None, :]).astype(jnp.bfloat16)
    token_sums = lax.dot_general(
        one_hot,
        branch_grads.reshape(tok_count, branches * width),
        (((0,), (0,)), ((), ())),
        preferred_element_type=jnp.float32,
    )
    summed = lax.psum_scatter(
        token_sums.reshape(vocabulary, branches, width), "seq", scatter_dimension=2, tiled=True
    )
    gathered = lax.all_gather(summed[:, :, None, :], "red", axis=2, tiled=True)
    weight_grad = (
        lax.dot_general(
            embedding.astype(jnp.float32),
            gathered.reshape(vocabulary, branches * red_count * piece),
            (((0,), (0,)), ((), ())),
            precision=precise_mode,
        )
        * scale_factor
    )
    return (
        output,
        filter_grad,
        branch_grads,
        weight_grad.reshape(width_rows, branches, red_count, piece),
    )


def solution(mesh):
    in_specs = (
        P("seq"),
        P(None, "red"),
        P("red", None, None, "seq"),
        P("seq", "red"),
        P("seq", "red"),
    )
    out_specs = (
        P("seq", "red"),
        P("seq", "red"),
        P("seq", None, "red"),
        P("red", None, None, "seq"),
    )
    return jax.shard_map(shards, mesh=mesh, in_specs=in_specs, out_specs=out_specs, check_vma=False)
```

profile of v0, /device:TPU:0, one launch (start us, length us, event | category | flops | bytes accessed | tf_op | source)
XLA Modules:
  0.0 223.0 jit_solution(11435874289733762096)
XLA Ops:
  8.4 2.6 %fusion.2 = f32[512,3,4,32]{0,3,2,1:T(8,128)} fusion(bf16[512,1024]{1,0:T(8,128)(2,1)S(1)} %copy-done, bf16[1024,3,4,32]{0,3,2,1:T(8,128)(2,1)} %param.7), kind=kOutput, calls=%fused_computation.10 | convolution fusion | flops 402653184 | bytes 2621440 | tf_op jit(solution)/shard_map/dot_general | solution.py:108
  11.7 46.1 %all-reduce.4.cloned.1.call-done = f32[512,3,4,32]{0,3,2,1:T(8,128)} async-done(((f32[512,3,4,32]{0,3,2,1:T(8,128)}), f32[512,3,4,32]{0,3,2,1:T(8,128)}) %all-reduce.4.cloned.1.call-update) | async-done | bytes 786448
  60.4 24.8 %all-gather.3.cloned.1.call-done = f32[512,3,1,256]{0,2,1,3:T(1,128)} async-done(((f32[512,3,1,32]{0,2,1,3:T(1,128)}), f32[512,3,1,256]{0,2,1,3:T(1,128)}) %all-gather.3.cloned.1.call-update) | async-done | bytes 1572880 | tf_op jit(solution)/shard_map/all_gather | solution.py:115
  85.2 4.7 %copy.121 = f32[512,3,1,256]{3,1,0,2:T(4,128)S(1)} copy(f32[512,3,1,256]{0,2,1,3:T(1,128)} %all-gather.3.cloned.1.call-done) | data formatting | bytes 3145728 | tf_op jit(solution)/shard_map/all_gather | solution.py:115
  89.9 1.6 gather_fusion
  95.9 3.5 %all-to-all-start = ((f32[128,3,256]{0,1,2:T(4,128)}), f32[128,3,256]{0,1,2:T(4,128)S(1)}, u32[]{:S(2)}, u32[]{:S(2)}) async-start(f32[128,3,256]{0,1,2:T(4,128)} %copy.123), calls=%async_computation | async-start | bytes 1048576 | tf_op jit(solution)/shard_map/all_to_all | solution.py:124
  100.0 9.0 %all-to-all-done = f32[128,3,256]{0,1,2:T(4,128)S(1)} async-done(((f32[128,3,256]{0,1,2:T(4,128)}), f32[128,3,256]{0,1,2:T(4,128)S(1)}, u32[]{:S(2)}, u32[]{:S(2)}) %all-to-all-start) | async-done | bytes 393248 | tf_op jit(solution)/shard_map/all_to_all | solution.py:124
  109.7 1.6 fusion.16
  111.3 1.9 multiply_subtract_fusion.3
  113.2 1.7 fusion.12
  115.0 1.7 fusion.8
  116.7 1.8 fusion.1
  118.5 1.8 fusion
  122.9 1.6 fusion.34
  124.5 1.6 fusion.32
  127.7 2.0 subtract_bitcast_fusion
  129.6 1.6 fusion.4
  131.2 1.6 fusion.6
  133.9 2.3 %reshape.135 = f32[1024,3,32]{2,1,0:T(4,128)S(1)} reshape(f32[16,64,96]{2,1,0:T(8,128)} %copy.148) | data formatting | bytes 786432 | tf_op jit(solution)/shard_map/div | solution.py:97
  137.5 10.7 %all_to_all.33 = f32[8,1,12288]{2,1,0:T(1,128)S(1)} all-to-all(f32[8,1,12288]{2,1,0:T(1,128)S(1)} %reshape.139), channel_id=1, replica_groups=mesh['seq'=8,'red'=4] {'seq'}, dimensions={0} | all-to-all | bytes 786432 | tf_op jit(solution)/shard_map/all_to_all | solution.py:126
  154.9 1.6 fusion.21
  158.7 35.4 %reduce-scatter.5.cloned.1.call-done = f32[512,3,32]{0,2,1:T(8,128)} async-done(((f32[512,3,256]{0,2,1:T(8,128)}), f32[512,3,32]{0,2,1:T(8,128)}) %reduce-scatter.5.cloned.1.call-update) | async-done | bytes 196624 | tf_op jit(solution)/shard_map/reduce_scatter | solution.py:142
  194.1 19.8 %all-gather = f32[512,3,128]{0,2,1:T(8,128)S(1)} all-gather(f32[512,3,32]{0,2,1:T(8,128)} %reduce-scatter.5.cloned.1.call-done), channel_id=2, replica_groups=mesh['seq'=8,'red'=4] {'red'}, dimensions={2}, use_global_device_ids=true | all-gather | bytes 983040 | tf_op jit(solution)/shard_map/all_gather | solution.py:145
  213.9 2.5 %convolution_multiply_fusion = f32[384,1024]{1,0:T(8,128)} fusion(f32[512,384]{0,1:T(8,128)S(1)} %bitcast.117, bf16[512,1024]{1,0:T(8,128)(2,1)S(1)} %copy-done), kind=kOutput, calls=%fused_computation.1 | convolution fusion | flops 2416312320 | bytes 3407872 | tf_op jit(solution)/shard_map/dot_general | solution.py:147
  (68 shorter events, 25.2 us)
Async XLA Ops:
  7.2 1.2 copy-start
  7.2 3.9 %copy-start.8 = (u32[32]{0:T(128)S(1)}, u32[32]{0:T(128)}, u32[]{:S(2)}) copy-start(u32[32]{0:T(128)} %constant.91) | copy-start | bytes 388
  7.2 50.6 %all-reduce.4.cloned.1.call-start = ((), (), s32[]{:S(2)}) async-start(), calls=%async_computation.5 | async-start | bytes 1572864
  11.0 49.2 %copy-start.6 = (f32[128,256]{1,0:T(8,128)S(1)}, f32[128,256]{1,0:T(8,128)}, u32[]{:S(2)}) copy-start(f32[128,256]{1,0:T(8,128)} %param.8) | copy-start | bytes 393220
  11.0 49.4 %copy-start.7 = (s32[128]{0:T(128)S(1)}, s32[128]{0:T(128)}, u32[]{:S(2)}) copy-start(s32[128]{0:T(128)} %param.5) | copy-start | bytes 1540
  11.0 74.2 %all-gather.3.cloned.1.call-start = ((), (), s32[]{:S(2)}) async-start(), calls=%async_computation.3 | async-start | bytes 1769472 | tf_op jit(solution)/shard_map/all_gather | solution.py:115
  89.9 4.0 %copy-start.4 = (f32[128,256]{1,0:T(8,128)S(1)}, f32[128,256]{1,0:T(8,128)}, u32[]{:S(2)}) copy-start(f32[128,256]{1,0:T(8,128)} %param.9) | copy-start | bytes 393220
  92.8 0.8 copy-start.1
  93.8 0.7 copy-start.2
  95.9 13.2 %all-to-all-start = ((f32[128,3,256]{0,1,2:T(4,128)}), f32[128,3,256]{0,1,2:T(4,128)S(1)}, u32[]{:S(2)}, u32[]{:S(2)}) async-start(f32[128,3,256]{0,1,2:T(4,128)} %copy.123), calls=%async_computation | async-start | bytes 1048576 | tf_op jit(solution)/shard_map/all_to_all | solution.py:124
  99.4 94.7 %reduce-scatter.5.cloned.1.call-start = ((), (), s32[]{:S(2)}) async-start(), calls=%async_computation.4 | async-start | bytes 1769472 | tf_op jit(solution)/shard_map/reduce_scatter | solution.py:142
  152.3 1.8 copy-start.5
  156.5 1.5 copy-start.3
Sparse Core Ops, SparseCore 0:
  11.2 46.5 all-reduce.3
  60.4 24.8 all-gather.2
  156.7 37.3 reduce-scatter.4
where the time goes:
time: 224 us; the launch traced here: 223 us
  waiting for transfers between devices  115 us (51%)
  blocking collectives  30.5 us (14%)
  matrix products  27.3 us (12%)
  local copies, waits for them, and re-layouts  22.8 us (10%)
  between operations  14.2 us (6%)
  other arithmetic  9.04 us (4%)
  starting transfers between devices  3.8 us (2%)
    unnamed x4, waiting for transfers between devices  46.1 us
    reduce_scatter x1, waiting for transfers between devices, shards(): lax.psum_scatter(token_sums.reshape(vocabulary, branches, width), 'seq',...  35.4 us
    all_gather x1, waiting for transfers between devices, shards(): full_table = lax.all_gather(own_table, 'seq', axis=3, tiled=True)  24.8 us
    all_gather x1, blocking collectives, shards(): gathered = lax.all_gather(summed[:, :, None, :], 'red', axis=2, tiled=True)  19.8 us
    all_to_all x1, blocking collectives, shards(): lax.all_to_all(results, 'seq', split_axis=0, concat_axis=2, tiled=True)  10.7 us
    unnamed x28, local copies, waits for them, and re-layouts  9.24 us
    all_to_all x1, waiting for transfers between devices, shards(): lax.all_to_all(stacked, 'seq', split_axis=2, concat_axis=0, tiled=True)  8.98 us
    all_gather x1, local copies, waits for them, and re-layouts, shards(): full_table = lax.all_gather(own_table, 'seq', axis=3, tiled=True)  4.65 us
  transfers between devices with their start and end apart: 4, of which 4 were waited for; matrix products, arithmetic and copies ran while one was open for 1% of the time, Pallas kernels for 0%

commit v1 on v0

--- a/solution.py
+++ b/solution.py
@@ -123,7 +123,10 @@
     stacked = jnp.stack([filters, inner, upstream], axis=1)
     whole_length = lax.all_to_all(stacked, "seq", split_axis=2, concat_axis=0, tiled=True)
     results = local_convolve(whole_length)
-    returned = lax.all_to_all(results, "seq", split_axis=0, concat_axis=2, tiled=True)
+    returned = jnp.concatenate(
+        lax.all_to_all(jnp.stack(jnp.split(results, lax.axis_size("seq"), axis=0)), "seq", 0, 0),
+        axis=2,
+    )
     conv = returned[:, 0]
     grad_inner = returned[:, 1]
     filter_raw = returned[:, 2]

time: 224 us -> 215 us (0.960)
  local copies, waits for them, and re-layouts: 22.8 us -> 16.7 us
  other arithmetic: 9.04 us -> 6.25 us
    unnamed x28 -> x25, local copies, waits for them, and re-layouts: 9.24 us -> 5.33 us
    div x2 -> x0, local copies, waits for them, and re-layouts: 3.26 us -> none  [local_convolve(): result = result.reshape(total, branch_count * narrow)[:length] / total]
  transfers between devices with their start and end apart: 4 -> 4, of which waited for: 4 -> 4; matrix products, arithmetic and copies ran while one was open for 1% -> 2% of each run, Pallas kernels for 0% -> 0%
where the time goes in v1:
time: 215 us; the launch traced here: 214 us
  waiting for transfers between devices  115 us (53%)
  blocking collectives  30.4 us (14%)
  matrix products  27.3 us (13%)
  local copies, waits for them, and re-layouts  16.7 us (8%)
  between operations  14.2 us (7%)
  other arithmetic  6.25 us (3%)
  starting transfers between devices  3.8 us (2%)
    unnamed x4, waiting for transfers between devices  46.1 us
    reduce_scatter x1, waiting for transfers between devices, shards(): lax.psum_scatter(token_sums.reshape(vocabulary, branches, width), 'seq',...  35.4 us
    all_gather x1, waiting for transfers between devices, shards(): full_table = lax.all_gather(own_table, 'seq', axis=3, tiled=True)  24.8 us
    all_gather x1, blocking collectives, shards(): gathered = lax.all_gather(summed[:, :, None, :], 'red', axis=2, tiled=True)  19.7 us
    all_to_all x1, blocking collectives, shards(): lax.all_to_all(jnp.stack(jnp.split(results, lax.axis_size('seq'), axis=0)...  10.7 us
    all_to_all x1, waiting for transfers between devices, shards(): lax.all_to_all(stacked, 'seq', split_axis=2, concat_axis=0, tiled=True)  8.98 us
    unnamed x25, local copies, waits for them, and re-layouts  5.33 us
    all_gather x1, local copies, waits for them, and re-layouts, shards(): full_table = lax.all_gather(own_table, 'seq', axis=3, tiled=True)  4.65 us
  transfers between devices with their start and end apart: 4, of which 4 were waited for; matrix products, arithmetic and copies ran while one was open for 2% of the time, Pallas kernels for 0%

profile of v1, /device:TPU:0, one launch (start us, length us, event | category | flops | bytes accessed | tf_op | source)
XLA Modules:
  0.0 214.1 jit_solution(14623932902881521271)
XLA Ops:
  8.4 2.6 %fusion.2 = f32[512,3,4,32]{0,3,2,1:T(8,128)} fusion(bf16[512,1024]{1,0:T(8,128)(2,1)S(1)} %copy-done, bf16[1024,3,4,32]{0,3,2,1:T(8,128)(2,1)} %param.7), kind=kOutput, calls=%fused_computation.10 | convolution fusion | flops 402653184 | bytes 2621440 | tf_op jit(solution)/shard_map/dot_general | solution.py:108
  11.7 46.1 %all-reduce.4.cloned.1.call-done = f32[512,3,4,32]{0,3,2,1:T(8,128)} async-done(((f32[512,3,4,32]{0,3,2,1:T(8,128)}), f32[512,3,4,32]{0,3,2,1:T(8,128)}) %all-reduce.4.cloned.1.call-update) | async-done | bytes 786448
  57.8 1.6 constant_dynamic-slice_fusion
  60.4 24.8 %all-gather.3.cloned.1.call-done = f32[512,3,1,256]{0,2,1,3:T(1,128)} async-done(((f32[512,3,1,32]{0,2,1,3:T(1,128)}), f32[512,3,1,256]{0,2,1,3:T(1,128)}) %all-gather.3.cloned.1.call-update) | async-done | bytes 1572880 | tf_op jit(solution)/shard_map/all_gather | solution.py:115
  85.2 4.7 %copy.145 = f32[512,3,1,256]{3,1,0,2:T(4,128)S(1)} copy(f32[512,3,1,256]{0,2,1,3:T(1,128)} %all-gather.3.cloned.1.call-done) | data formatting | bytes 3145728 | tf_op jit(solution)/shard_map/all_gather | solution.py:115
  89.9 1.6 gather_fusion
  94.6 3.5 %all-to-all-start = ((f32[128,3,256]{0,1,2:T(4,128)}), f32[128,3,256]{0,1,2:T(4,128)S(1)}, u32[]{:S(2)}, u32[]{:S(2)}) async-start(f32[128,3,256]{0,1,2:T(4,128)} %copy.147), calls=%async_computation | async-start | bytes 1048576 | tf_op jit(solution)/shard_map/all_to_all | solution.py:124
  98.7 9.0 %all-to-all-done = f32[128,3,256]{0,1,2:T(4,128)S(1)} async-done(((f32[128,3,256]{0,1,2:T(4,128)}), f32[128,3,256]{0,1,2:T(4,128)S(1)}, u32[]{:S(2)}, u32[]{:S(2)}) %all-to-all-start) | async-done | bytes 393248 | tf_op jit(solution)/shard_map/all_to_all | solution.py:124
  108.3 1.6 fusion.16
  109.9 1.9 multiply_subtract_fusion.3
  111.9 1.7 fusion.12
  113.7 1.7 fusion.8
  115.4 1.8 fusion.1
  117.2 1.8 fusion
  121.6 1.6 fusion.34
  123.2 1.6 fusion.32
  126.4 2.0 subtract_bitcast_fusion
  128.3 1.6 fusion.4
  129.9 1.6 fusion.6
  134.0 10.7 %all_to_all.20 = f32[8,128,3,32]{1,3,2,0:T(8,128)S(1)} all-to-all(f32[8,128,3,32]{1,3,2,0:T(8,128)S(1)} %constant_dynamic-update-slice_fusion), channel_id=1, replica_groups=mesh['seq'=8,'red'=4] {'seq'}, dimensions={0} | all-to-all | bytes 786432 | tf_op jit(solution)/shard_map/all_to_all | solution.py:127
  146.1 1.6 fusion.21
  149.9 35.4 %reduce-scatter.5.cloned.1.call-done = f32[512,3,32]{0,2,1:T(8,128)} async-done(((f32[512,3,256]{0,2,1:T(8,128)}), f32[512,3,32]{0,2,1:T(8,128)}) %reduce-scatter.5.cloned.1.call-update) | async-done | bytes 196624 | tf_op jit(solution)/shard_map/reduce_scatter | solution.py:145
  185.3 19.7 %all-gather = f32[512,3,128]{0,2,1:T(8,128)S(1)} all-gather(f32[512,3,32]{0,2,1:T(8,128)} %reduce-scatter.5.cloned.1.call-done), channel_id=2, replica_groups=mesh['seq'=8,'red'=4] {'red'}, dimensions={2}, use_global_device_ids=true | all-gather | bytes 983040 | tf_op jit(solution)/shard_map/all_gather | solution.py:148
  205.0 2.5 %convolution_multiply_fusion = f32[384,1024]{1,0:T(8,128)} fusion(f32[512,384]{0,1:T(8,128)S(1)} %bitcast.129, bf16[512,1024]{1,0:T(8,128)(2,1)S(1)} %copy-done), kind=kOutput, calls=%fused_computation.1 | convolution fusion | flops 2416312320 | bytes 3407872 | tf_op jit(solution)/shard_map/dot_general | solution.py:150
  (79 shorter events, 17.0 us)
Async XLA Ops:
  7.2 1.2 copy-start
  7.2 3.9 %copy-start.4 = (u32[32]{0:T(128)S(1)}, u32[32]{0:T(128)}, u32[]{:S(2)}) copy-start(u32[32]{0:T(128)} %constant.91) | copy-start | bytes 388
  7.2 50.6 %all-reduce.4.cloned.1.call-start = ((), (), s32[]{:S(2)}) async-start(), calls=%async_computation.5 | async-start | bytes 1572864
  11.0 49.2 %copy-start.2 = (f32[128,256]{1,0:T(8,128)S(1)}, f32[128,256]{1,0:T(8,128)}, u32[]{:S(2)}) copy-start(f32[128,256]{1,0:T(8,128)} %param.8) | copy-start | bytes 393220
  11.0 49.4 %copy-start.3 = (s32[128]{0:T(128)S(1)}, s32[128]{0:T(128)}, u32[]{:S(2)}) copy-start(s32[128]{0:T(128)} %param.5) | copy-start | bytes 1540
  11.0 74.2 %all-gather.3.cloned.1.call-start = ((), (), s32[]{:S(2)}) async-start(), calls=%async_computation.3 | async-start | bytes 1769472 | tf_op jit(solution)/shard_map/all_gather | solution.py:115
  89.9 3.2 %copy-start.1 = (f32[128,256]{1,0:T(8,128)S(1)}, f32[128,256]{1,0:T(8,128)}, u32[]{:S(2)}) copy-start(f32[128,256]{1,0:T(8,128)} %param.9) | copy-start | bytes 393220
  94.6 13.2 %all-to-all-start = ((f32[128,3,256]{0,1,2:T(4,128)}), f32[128,3,256]{0,1,2:T(4,128)S(1)}, u32[]{:S(2)}, u32[]{:S(2)}) async-start(f32[128,3,256]{0,1,2:T(4,128)} %copy.147), calls=%async_computation | async-start | bytes 1048576 | tf_op jit(solution)/shard_map/all_to_all | solution.py:124
  98.1 87.2 %reduce-scatter.5.cloned.1.call-start = ((), (), s32[]{:S(2)}) async-start(), calls=%async_computation.4 | async-start | bytes 1769472 | tf_op jit(solution)/shard_map/reduce_scatter | solution.py:145
Sparse Core Ops, SparseCore 0:
  11.2 46.5 all-reduce.3
  60.4 24.8 all-gather.2
  147.9 37.3 reduce-scatter.4
